TPU v7x, 256 devices: a whole 4x4x8 slice. The times are simulated.
256 devices in a mesh: leaf: 32 (over y, z), panel: 8 (over x, core).
Axes of the slice: x: 4, y: 4, z: 8, core: 2. Of those that a mesh axis runs over, the one named last changes fastest.
Arguments:
- child_front: float32 [32, 2, 8, 128, 2048], P('leaf', None, 'panel'), as said below
- parent_entries: float32 [32, 4, 8, 128, 512], P('leaf', None, 'panel'), as said below
- parent_of: int32 [32], replicated, may hold values from 0 to 31
- owner_slot: int32 [32], replicated, may hold values from 0 to 31, each once
- front_blocks: int32 [32], replicated, may hold values from 8 to 32, as said below
- block_lists: int32 [32, 8], replicated, may hold values from 0 to 31, as said below
Outputs:
- child_factor: float32 [32, 2, 8, 128, 1024], P('leaf', None, 'panel')
- parent_factor: float32 [32, 4, 8, 128, 512], P('leaf', None, 'panel')
Inputs may be any that keep to these rules, and one draw needn't show every extreme that they name: `front_blocks`: each entry is a multiple of the panel axis size; the largest equals 32. `block_lists`: the entries of a row are distinct, each below front_blocks of the child's parent, and entry k leaves the same remainder as k when divided by the panel axis size. `child_front`: symmetric, with a positive definite leading block of every front. `parent_entries`: the leading 512 rows form a symmetric positive definite block.
All inputs are finite; a program needn't handle non-finite values.
Results may differ from a plain program's by a relative error of at most 0.00044.
Values may be sent and summed in bfloat16 or wider, within the bound.
No kernel may reach another device: no remote copies, remote signals or barrier semaphores. Data moves between devices by JAX's collectives and lax.ppermute only.
A program may use at most 128 MiB of HBM per device.

v0:
```python
import jax
import jax.numpy as jnp
from jax import lax
from jax.sharding import PartitionSpec as P

BLK = 128
PANEL = 512
WC = 2048
PC = 1024
CBB = 8


def place_columns(block_rows, block_map):
    count_in = block_rows.shape[0]
    row_slots = block_rows.shape[1]
    pivot_blocks = PANEL // BLK
    onehot = (block_map[:, :, None] == jnp.arange(pivot_blocks)[None, None, :]).astype(jnp.bfloat16)
    split_blocks = block_rows.reshape(count_in, row_slots, BLK, CBB, BLK)
    placed = jnp.einsum(
        "muvkc,mkb->muvbc", split_blocks, onehot, preferred_element_type=jnp.float32
    )
    return placed.reshape(count_in, row_slots, BLK, PANEL)


def place_rows(assembled, placed, block_map, destination, panel_count, panel_index, leaf_index):
    count_in = placed.shape[0]
    row_slots = placed.shape[1]
    parent_slots = assembled.shape[0]
    grouped = block_map.reshape(count_in, row_slots, panel_count)
    pick = (jnp.arange(panel_count) == panel_index).astype(jnp.int32)
    row_blocks = jnp.sum(grouped * pick[None, None, :], axis=2)
    target = row_blocks[:, :, None] // panel_count == jnp.arange(parent_slots)[None, None, :]
    target = jnp.logical_and(target, (destination == leaf_index)[:, None, None]).astype(jnp.float32)
    return assembled + jnp.einsum("muvx,mut->tvx", placed, target, precision=lax.Precision.HIGHEST)


def on_device(child_front, parent_entries, parent_of, owner_slot, front_blocks, block_lists):
    panel_count = lax.axis_size("panel")
    panel_index = lax.axis_index("panel")
    leaf_index = lax.axis_index("leaf")
    row_slots = child_front.shape[1]
    parent_slots = parent_entries.shape[1]
    local_rows = child_front.reshape(row_slots * BLK, WC)
    factors = []
    for first_col in range(0, PC, PANEL):
        trailing = first_col + PANEL
        column = local_rows[:, first_col:trailing]
        gathered = lax.all_gather(
            column.reshape(row_slots, 1, BLK, PANEL), "panel", axis=1, tiled=True
        )
        gathered = gathered.reshape(WC, PANEL)
        pivot_block = jnp.linalg.cholesky(gathered[first_col:trailing])
        all_rows = jax.scipy.linalg.solve_triangular(pivot_block, gathered.T, lower=True).T
        all_rows = jnp.where(jnp.arange(WC)[:, None] >= first_col, all_rows, 0.0)
        own_rows = lax.dynamic_slice_in_dim(
            all_rows.reshape(row_slots, panel_count, BLK, PANEL), panel_index, 1, 1
        )
        own_rows = own_rows.reshape(row_slots * BLK, PANEL)
        update = jnp.dot(own_rows, all_rows[trailing:].T, precision=lax.Precision.HIGHEST)
        local_rows = jnp.concatenate(
            [local_rows[:, :trailing], local_rows[:, trailing:] - update], axis=1
        )
        factors.append(own_rows)
    child_factor = jnp.concatenate(factors, axis=1).reshape(1, row_slots, 1, BLK, PC)
    first_cb = PC // (BLK * panel_count)
    contribution = local_rows.reshape(row_slots, BLK, WC)[first_cb:, :, PC:].astype(jnp.bfloat16)
    parent_hits = (parent_of[:, None] == jnp.arange(owner_slot.shape[0])[None, :]).astype(jnp.int32)
    slot_of_child = jnp.sum(parent_hits * owner_slot[None, :], axis=1)
    live_mine = jnp.sum(jnp.where(owner_slot == leaf_index, front_blocks, 0))
    entries = parent_entries.reshape(parent_slots, BLK, PANEL)
    global_block = jnp.arange(parent_slots) * panel_count + panel_index
    initial = jnp.where((global_block < live_mine)[:, None, None], entries, 0.0)
    placed = place_columns(
        lax.all_gather(contribution[None], "leaf", axis=0, tiled=True), block_lists
    )
    assembled = place_rows(
        initial, placed, block_lists, slot_of_child, panel_count, panel_index, leaf_index
    )
    stacked = lax.all_gather(assembled[0], "panel", axis=0, tiled=True)
    pivot_block = jnp.linalg.cholesky(stacked[:PANEL])
    parent_rows = assembled.reshape(parent_slots * BLK, PANEL)
    parent_factor = jax.scipy.linalg.solve_triangular(pivot_block, parent_rows.T, lower=True).T
    return (child_factor, parent_factor.reshape(1, parent_slots, 1, BLK, PANEL))


def solution(mesh):
    in_specs = (
        P("leaf", None, "panel", None, None),
        P("leaf", None, "panel", None, None),
        P(),
        P(),
        P(),
        P(),
    )
    out_specs = (P("leaf", None, "panel", None, None), P("leaf", None, "panel", None, None))
    return jax.shard_map(
        on_device, mesh=mesh, in_specs=in_specs, out_specs=out_specs, check_vma=False
    )
```

profile of v0, /device:TPU:1, one launch (start us, length us, event | category | flops | bytes accessed | tf_op | source)
XLA Modules:
  0.0 736.7 jit_solution(10436099563935229929)
XLA Ops:
  7.2 1.9 slice.189
  9.2 40.2 %all-gather.7.cloned.1.call-done = f32[2,8,128,512]{3,2,0,1:T(8,128)} async-done(((f32[2,1,128,512]{3,2,0,1:T(8,128)}), f32[2,8,128,512]{3,2,0,1:T(8,128)}) %all-gather.7.cloned.1.call-update) | async-done | bytes 4194320 | tf_op jit(solution)/shard_map/all_gather | solution.py:48
  49.3 5.4 copy.47
  54.8 4.1 copy.89
  58.9 1.9 copy-done
  61.3 1.4 fusion.58
  62.7 11.7 %cholesky.374 = f32[128,128]{1,0:T(8,128)S(1)} custom-call(f32[128,128]{1,0:T(8,128)S(1)} %cholesky.586), custom_call_target="Cholesky" | custom-call | tf_op jit(solution)/shard_map/jit(cholesky)/cholesky | solution.py:52
  74.5 9.8 %custom-call.35 = f32[1,128,128]{1,2,0:T(8,128)S(1)} custom-call(f32[1,128,128]{2,1,0:T(8,128)S(1)} %get-tuple-element.103), custom_call_target="InvertDiagBlocksLowerTriangular" | custom-call | tf_op jit(solution)/shard_map/jit(cholesky)/cholesky | solution.py:52
  85.1 11.9 %cholesky.393 = f32[128,128]{1,0:T(8,128)S(1)} custom-call(f32[128,128]{1,0:T(8,128)S(1)} %cholesky.590), custom_call_target="Cholesky" | custom-call | tf_op jit(solution)/shard_map/jit(cholesky)/cholesky | solution.py:52
  97.0 9.8 %custom-call.36 = f32[1,128,128]{1,2,0:T(8,128)S(1)} custom-call(f32[1,128,128]{2,1,0:T(8,128)S(1)} %get-tuple-element.100), custom_call_target="InvertDiagBlocksLowerTriangular" | custom-call | tf_op jit(solution)/shard_map/jit(cholesky)/cholesky | solution.py:52
  107.5 11.7 %cholesky.414 = f32[128,128]{1,0:T(8,128)S(1)} custom-call(f32[128,128]{1,0:T(8,128)S(1)} %cholesky.595), custom_call_target="Cholesky" | custom-call | tf_op jit(solution)/shard_map/jit(cholesky)/cholesky | solution.py:52
  119.9 9.8 %custom-call.37 = f32[1,128,128]{1,2,0:T(8,128)S(1)} custom-call(f32[1,128,128]{2,1,0:T(8,128)S(1)} %get-tuple-element.97), custom_call_target="InvertDiagBlocksLowerTriangular" | custom-call | tf_op jit(solution)/shard_map/jit(cholesky)/cholesky | solution.py:52
  130.3 12.1 %cholesky.431 = f32[128,128]{1,0:T(8,128)S(1)} custom-call(f32[128,128]{1,0:T(8,128)S(1)} %convolution_subtract_fusion.15), custom_call_target="Cholesky" | custom-call | tf_op jit(solution)/shard_map/jit(cholesky)/cholesky | solution.py:52
  146.6 7.9 %while.6 = (s32[]{:T(128)}, f32[512,512]{1,0:T(8,128)S(1)}, s32[4,2]{0,1:T(2,128)S(1)}, f32[4,128,128]{2,1,0:T(8,128)S(1)}, s32[]{:T(128)}) while((s32[]{:T(128)}, f32[512,512]{1,0:T(8,128)S(1)}, s32[4,2]{0,1:T(2,128)S(1)}, f32[4,128,128]{2,1,0:T(8,128)S(1)}, s32[]{:T(128)}) %tuple.88), condition=%wide.while_cond, body=%wide.while_body.sunk | while | flops 2 | bytes 131181 | solution.py:53
  154.5 39.3 %custom-call.38 = f32[4,128,128]{1,2,0:T(8,128)S(1)} custom-call(f32[4,128,128]{2,1,0:T(8,128)S(1)} %get-tuple-element.26), custom_call_target="InvertDiagBlocksLowerTriangular" | custom-call | tf_op jit(solution)/shard_map/jit(_solve_triangular)/triangular_solve | solution.py:53
  193.8 2.4 fusion.53
  196.2 2.3 convolution_subtract_fusion.3
  201.9 2.0 fusion.27
  207.6 4.0 fusion.144
  213.6 33.6 %all-gather.9.cloned.1.call-done = f32[2,8,128,512]{3,2,0,1:T(8,128)} async-done(((f32[2,1,128,512]{3,2,0,1:T(8,128)}), f32[2,8,128,512]{3,2,0,1:T(8,128)}) %all-gather.9.cloned.1.call-update) | async-done | bytes 4194320 | tf_op jit(solution)/shard_map/all_gather | solution.py:48
  247.3 5.4 copy.50
  252.7 4.1 copy.88
  256.9 1.9 copy-done.2
  259.9 1.6 copy.51
  261.4 1.4 fusion.57
  263.9 11.7 %cholesky.446 = f32[128,128]{1,0:T(8,128)S(1)} custom-call(f32[128,128]{1,0:T(8,128)S(1)} %cholesky.599), custom_call_target="Cholesky" | custom-call | tf_op jit(solution)/shard_map/jit(cholesky)/cholesky | solution.py:52
  275.7 9.8 %custom-call.39 = f32[1,128,128]{1,2,0:T(8,128)S(1)} custom-call(f32[1,128,128]{2,1,0:T(8,128)S(1)} %get-tuple-element.93), custom_call_target="InvertDiagBlocksLowerTriangular" | custom-call | tf_op jit(solution)/shard_map/jit(cholesky)/cholesky | solution.py:52
  288.1 12.1 %cholesky.465 = f32[128,128]{1,0:T(8,128)S(1)} custom-call(f32[128,128]{1,0:T(8,128)S(1)} %cholesky.603), custom_call_target="Cholesky" | custom-call | tf_op jit(solution)/shard_map/jit(cholesky)/cholesky | solution.py:52
  301.5 9.8 %custom-call.40 = f32[1,128,128]{1,2,0:T(8,128)S(1)} custom-call(f32[1,128,128]{2,1,0:T(8,128)S(1)} %get-tuple-element.90), custom_call_target="InvertDiagBlocksLowerTriangular" | custom-call | tf_op jit(solution)/shard_map/jit(cholesky)/cholesky | solution.py:52
  312.9 11.7 %cholesky.486 = f32[128,128]{1,0:T(8,128)S(1)} custom-call(f32[128,128]{1,0:T(8,128)S(1)} %cholesky.608), custom_call_target="Cholesky" | custom-call | tf_op jit(solution)/shard_map/jit(cholesky)/cholesky | solution.py:52
  325.4 9.8 %custom-call.41 = f32[1,128,128]{1,2,0:T(8,128)S(1)} custom-call(f32[1,128,128]{2,1,0:T(8,128)S(1)} %get-tuple-element.87), custom_call_target="InvertDiagBlocksLowerTriangular" | custom-call | tf_op jit(solution)/shard_map/jit(cholesky)/cholesky | solution.py:52
  336.6 11.9 %cholesky.503 = f32[128,128]{1,0:T(8,128)S(1)} custom-call(f32[128,128]{1,0:T(8,128)S(1)} %convolution_subtract_fusion.14), custom_call_target="Cholesky" | custom-call | tf_op jit(solution)/shard_map/jit(cholesky)/cholesky | solution.py:52
  352.9 11.4 %while.7 = (s32[]{:T(128)}, f32[512,512]{1,0:T(8,128)}, s32[4,2]{0,1:T(2,128)S(1)}, f32[4,128,128]{2,1,0:T(8,128)S(1)}, s32[]{:T(128)}) while((s32[]{:T(128)}, f32[512,512]{1,0:T(8,128)}, s32[4,2]{0,1:T(2,128)S(1)}, f32[4,128,128]{2,1,0:T(8,128)S(1)}, s32[]{:T(128)}) %tuple.105), condition=%wide.while_cond.clone, body=%wide.while_body.clone.sunk | while | flops 2 | bytes 131181 | solution.py:53
  353.5 2.2 bitcast_dynamic-update-slice_fusion.8
  356.4 2.2 bitcast_dynamic-update-slice_fusion.8
  359.3 2.2 bitcast_dynamic-update-slice_fusion.8
  362.1 2.2 bitcast_dynamic-update-slice_fusion.8
  364.3 39.3 %custom-call.42 = f32[4,128,128]{1,2,0:T(8,128)S(1)} custom-call(f32[4,128,128]{2,1,0:T(8,128)S(1)} %get-tuple-element.27), custom_call_target="InvertDiagBlocksLowerTriangular" | custom-call | tf_op jit(solution)/shard_map/jit(_solve_triangular)/triangular_solve | solution.py:53
  403.6 2.4 fusion.51
  406.0 2.3 convolution_subtract_fusion.2
  409.4 2.1 convolution_subtract_fusion
  412.6 3.0 fusion.24
  419.3 1.9 fusion.46
  422.6 1.5 copy.53
  425.7 94.6 %all-gather.11.cloned.1.call-done = bf16[32,128,1024]{2,1,0:T(8,128)(2,1)} async-done(((bf16[1,128,1024]{2,1,0:T(8,128)(2,1)}), bf16[32,128,1024]{2,1,0:T(8,128)(2,1)}) %all-gather.11.cloned.1.call-update) | async-done | bytes 8388624 | tf_op jit(solution)/shard_map/all_gather | solution.py:74
  520.3 8.8 %copy.69 = bf16[512,8,8,128]{3,2,1,0:T(8,128)(2,1)} copy(bf16[512,8,8,128]{3,1,2,0:T(8,128)(2,1)} %bitcast.259) | data formatting | bytes 16777216
  529.1 8.9 %fusion.4 = f32[32,1,128,4,128]{4,3,2,0,1:T(4,128)} fusion(s32[32,8]{1,0:T(8,128)S(1)} %copy.54, bf16[32,128,8,128]{3,2,1,0:T(8,128)(2,1)} %bitcast.244), kind=kOutput, calls=%fused_computation.10 | convolution fusion | flops 33555456 | bytes 16778240 | tf_op jit(solution)/shard_map/muvkc,mkb->muvbc/dot_general | solution.py:19
  538.0 10.3 %reshape.264 = f32[32,128,512]{2,1,0:T(8,128)} reshape(f32[32,1,128,4,128]{4,3,2,0,1:T(4,128)} %fusion.4) | data formatting | bytes 16777216 | tf_op jit(solution)/shard_map/reshape.65
  548.2 10.4 %fusion.2 = f32[4,128,512]{2,0,1:T(4,128)S(1)} fusion(f32[32,128,512]{2,1,0:T(8,128)} %reshape.264, s32[32]{0:T(128)S(1)} %get-tuple-element.112, pred[32]{0:T(512)(128)(4,1)S(1)} %broadcast_compare_fusion), kind=kOutput, calls=%fused_computation.8 | convolution fusion | flops 100663552 | bytes 9437344 | tf_op jit(solution)/shard_map/muvx,mut->tvx/dot_general | solution.py:34
  565.5 24.5 %all-gather.13.cloned.1.call-done = f32[1,1024,512]{1,2,0:T(8,128)} async-done(((f32[1,128,512]{1,2,0:T(8,128)}), f32[1,1024,512]{1,2,0:T(8,128)}) %all-gather.13.cloned.1.call-update) | async-done | bytes 2097168 | tf_op jit(solution)/shard_map/all_gather | solution.py:79
  591.7 1.4 fusion.55
  593.1 11.7 %cholesky.518 = f32[128,128]{1,0:T(8,128)S(1)} custom-call(f32[128,128]{1,0:T(8,128)S(1)} %cholesky.612), custom_call_target="Cholesky" | custom-call | tf_op jit(solution)/shard_map/jit(cholesky)/cholesky | solution.py:80
  605.0 9.8 %custom-call.43 = f32[1,128,128]{1,2,0:T(8,128)S(1)} custom-call(f32[1,128,128]{2,1,0:T(8,128)S(1)} %get-tuple-element.83), custom_call_target="InvertDiagBlocksLowerTriangular" | custom-call | tf_op jit(solution)/shard_map/jit(cholesky)/cholesky | solution.py:80
  615.5 11.7 %cholesky.537 = f32[128,128]{1,0:T(8,128)S(1)} custom-call(f32[128,128]{1,0:T(8,128)S(1)} %cholesky.616), custom_call_target="Cholesky" | custom-call | tf_op jit(solution)/shard_map/jit(cholesky)/cholesky | solution.py:80
  628.6 10.0 %custom-call.44 = f32[1,128,128]{1,2,0:T(8,128)S(1)} custom-call(f32[1,128,128]{2,1,0:T(8,128)S(1)} %get-tuple-element.80), custom_call_target="InvertDiagBlocksLowerTriangular" | custom-call | tf_op jit(solution)/shard_map/jit(cholesky)/cholesky | solution.py:80
  639.2 11.7 %cholesky.558 = f32[128,128]{1,0:T(8,128)S(1)} custom-call(f32[128,128]{1,0:T(8,128)S(1)} %cholesky.621), custom_call_target="Cholesky" | custom-call | tf_op jit(solution)/shard_map/jit(cholesky)/cholesky | solution.py:80
  651.6 9.8 %custom-call.45 = f32[1,128,128]{1,2,0:T(8,128)S(1)} custom-call(f32[1,128,128]{2,1,0:T(8,128)S(1)} %get-tuple-element.77), custom_call_target="InvertDiagBlocksLowerTriangular" | custom-call | tf_op jit(solution)/shard_map/jit(cholesky)/cholesky | solution.py:80
  662.0 11.9 %cholesky.575 = f32[128,128]{1,0:T(8,128)S(1)} custom-call(f32[128,128]{1,0:T(8,128)S(1)} %convolution_subtract_fusion.13), custom_call_target="Cholesky" | custom-call | tf_op jit(solution)/shard_map/jit(cholesky)/cholesky | solution.py:80
  677.4 8.5 %while.5 = (s32[]{:T(128)}, f32[512,512]{1,0:T(8,128)S(1)}, s32[4,2]{0,1:T(2,128)S(1)}, f32[4,128,128]{2,1,0:T(8,128)S(1)}, s32[]{:T(128)}) while((s32[]{:T(128)}, f32[512,512]{1,0:T(8,128)S(1)}, s32[4,2]{0,1:T(2,128)S(1)}, f32[4,128,128]{2,1,0:T(8,128)S(1)}, s32[]{:T(128)}) %tuple.106), condition=%wide.while_cond.1, body=%wide.while_body.1.sunk | while | flops 2 | bytes 131181 | solution.py:82
  678.1 1.4 bitcast_dynamic-update-slice_fusion.6
  680.2 1.4 bitcast_dynamic-update-slice_fusion.6
  682.3 1.4 bitcast_dynamic-update-slice_fusion.6
  684.4 1.4 bitcast_dynamic-update-slice_fusion.6
  685.9 39.3 %custom-call.27 = f32[4,128,128]{1,2,0:T(8,128)S(1)} custom-call(f32[4,128,128]{2,1,0:T(8,128)S(1)} %get-tuple-element.19), custom_call_target="InvertDiagBlocksLowerTriangular" | custom-call | tf_op jit(solution)/shard_map/jit(_solve_triangular)/triangular_solve | solution.py:82
  (168 shorter events, 64.9 us)
Async XLA Ops:
  7.2 42.2 %all-gather.7.cloned.1.call-start = ((), (), s32[]{:S(2)}) async-start(), calls=%async_computation | async-start | bytes 4718592 | tf_op jit(solution)/shard_map/all_gather | solution.py:48
  9.1 238.2 %all-gather.9.cloned.1.call-start = ((), (), s32[]{:S(2)}) async-start(), calls=%async_computation.1 | async-start | bytes 4718592 | tf_op jit(solution)/shard_map/all_gather | solution.py:48
  58.9 1.9 copy-start
  193.8 5.7 copy-start.1
  206.0 1.6 copy-start.8
  207.4 5.1 copy-start.4
  212.5 307.8 %all-gather.11.cloned.1.call-start = ((), (), s32[]{:S(2)}) async-start(), calls=%async_computation.2 | async-start | bytes 8650752 | tf_op jit(solution)/shard_map/all_gather | solution.py:74
  256.9 1.9 copy-start.2
  262.9 1.0 copy-start.7
  403.6 5.8 copy-start.3
  418.8 2.4 copy-start.6
  418.9 3.7 copy-start.9
  419.2 5.0 copy-start.10
  419.2 5.0 copy-start.11
  419.3 6.3 copy-start.12
  422.5 167.6 %all-gather.13.cloned.1.call-start = ((), (), s32[]{:S(2)}) async-start(), calls=%async_computation.3 | async-start | bytes 2359296 | tf_op jit(solution)/shard_map/all_gather | solution.py:79
  558.7 3.5 copy-start.5
Sparse Core Ops, SparseCore 0:
  10.4 38.8 all-gather.6
  212.6 34.6 all-gather.8
  422.6 97.6 all-gather.10
  562.3 27.6 all-gather.12
where the time goes:
time: 747 us; the launch traced here: 737 us
  other arithmetic  369 us (49%)
  waiting for transfers between devices  193 us (26%)
  local copies, waits for them, and re-layouts  90.3 us (12%)
  matrix products  61.6 us (8%)
  between operations  22.8 us (3%)
    another operation x29, other arithmetic, on_device(): pivot_block = jnp.linalg.cholesky(gathered[first_col:trailing])  159 us
    all_gather x1, waiting for transfers between devices, on_device(): lax.all_gather(contribution[None], 'leaf', axis=0, tiled=True)  94.6 us
    another operation x5, other arithmetic, on_device(): jax.scipy.linalg.solve_triangular(pivot_block, gathered.T, lower=True)  79.9 us
    another operation x15, other arithmetic, on_device(): pivot_block = jnp.linalg.cholesky(stacked[:PANEL])  79.4 us
    all_gather x2, waiting for transfers between devices, on_device(): lax.all_gather(column.reshape(row_slots, 1, BLK, PANEL), 'panel', axis=1,...  73.8 us
    another operation x2, other arithmetic, on_device(): jax.scipy.linalg.solve_triangular(pivot_block, parent_rows.T, lower=True)  39.4 us
    unnamed x34, local copies, waits for them, and re-layouts  27 us
    all_gather x1, waiting for transfers between devices, on_device(): stacked = lax.all_gather(assembled[0], 'panel', axis=0, tiled=True)  24.5 us
  transfers between devices with their start and end apart: 4, of which 4 were waited for; matrix products, arithmetic and copies ran while one was open for 1% of the time, Pallas kernels for 0%

commit v1 on v0

--- a/solution.py
+++ b/solution.py
@@ -2,6 +2,7 @@
 import jax.numpy as jnp
 from jax import lax
 from jax.sharding import PartitionSpec as P
+from jax.lax import all_to_all, axis_size
 
 BLK = 128
 PANEL = 512
@@ -45,9 +46,12 @@
     for first_col in range(0, PC, PANEL):
         trailing = first_col + PANEL
         column = local_rows[:, first_col:trailing]
-        gathered = lax.all_gather(
-            column.reshape(row_slots, 1, BLK, PANEL), "panel", axis=1, tiled=True
-        )
+        point = column.reshape(row_slots, 1, BLK, PANEL)
+        bank = []
+        for _ in range(axis_size("panel")):
+            bank.append(point)
+        arr_next = jnp.stack(bank, 0)
+        gathered = jnp.concatenate(all_to_all(arr_next, "panel", split_axis=0, concat_axis=0), 1)
         gathered = gathered.reshape(WC, PANEL)
         pivot_block = jnp.linalg.cholesky(gathered[first_col:trailing])
         all_rows = jax.scipy.linalg.solve_triangular(pivot_block, gathered.T, lower=True).T

time: 747 us -> 786 us (1.052)
  waiting for transfers between devices: 193 us -> 216 us
  starting transfers between devices: 0.16 us -> 13 us
    all_to_all x0 -> x2, waiting for transfers between devices: none -> 96.8 us  [on_device(): all_to_all(arr_next, 'panel', split_axis=0, concat_axis=0)]
    all_gather x2 -> x0, waiting for transfers between devices: 73.8 us -> none  [on_device(): lax.all_gather(column.reshape(row_slots, 1, BLK, PANEL), 'panel', axis=1,...]
    another operation x13 -> x19, local copies, waits for them, and re-layouts: 18.7 us -> 35.5 us
    reshape x0 -> x2, local copies, waits for them, and re-layouts: none -> 13.2 us  [on_device(): jnp.concatenate(all_to_all(arr_next, 'panel', split_axis=0, concat_axis=0...]
    all_to_all x0 -> x2, starting transfers between devices: none -> 12.9 us  [on_device(): all_to_all(arr_next, 'panel', split_axis=0, concat_axis=0)]
    unnamed x34 -> x28, local copies, waits for them, and re-layouts: 27 us -> 14.8 us
    all_gather x2 -> x0, local copies, waits for them, and re-layouts: 10.9 us -> none  [on_device(): lax.all_gather(column.reshape(row_slots, 1, BLK, PANEL), 'panel', axis=1,...]
where the time goes in v1:
time: 786 us; the launch traced here: 780 us
  other arithmetic  368 us (47%)
  waiting for transfers between devices  216 us (27%)
  local copies, waits for them, and re-layouts  98.1 us (12%)
  matrix products  61.6 us (8%)
  between operations  23 us (3%)
  starting transfers between devices  13 us (2%)
    another operation x29, other arithmetic, on_device(): pivot_block = jnp.linalg.cholesky(gathered[first_col:trailing])  158 us
    all_to_all x2, waiting for transfers between devices, on_device(): all_to_all(arr_next, 'panel', split_axis=0, concat_axis=0)  96.8 us
    all_gather x1, waiting for transfers between devices, on_device(): lax.all_gather(contribution[None], 'leaf', axis=0, tiled=True)  94.5 us
    another operation x5, other arithmetic, on_device(): jax.scipy.linalg.solve_triangular(pivot_block, gathered.T, lower=True)  80.2 us
    another operation x15, other arithmetic, on_device(): pivot_block = jnp.linalg.cholesky(stacked[:PANEL])  79.4 us
    another operation x2, other arithmetic, on_device(): jax.scipy.linalg.solve_triangular(pivot_block, parent_rows.T, lower=True)  39.4 us
    all_gather x1, waiting for transfers between devices, on_device(): stacked = lax.all_gather(assembled[0], 'panel', axis=0, tiled=True)  24.5 us
    another operation x14, matrix products, on_device(): jax.scipy.linalg.solve_triangular(pivot_block, gathered.T, lower=True)  24 us
  transfers between devices with their start and end apart: 4, of which 4 were waited for; matrix products, arithmetic and copies ran while one was open for 1% of the time, Pallas kernels for 0%

profile of v1, /device:TPU:1, one launch (start us, length us, event | category | flops | bytes accessed | tf_op | source)
XLA Modules:
  0.0 780.3 jit_solution(2685522328373855479)
XLA Ops:
  8.5 3.0 stack.6
  11.5 7.7 all-to-all-start
  19.2 48.9 %all-to-all-done = f32[8,2,1,128,512]{3,1,4,2,0:T(2,128)} async-done(((f32[8,2,1,128,512]{3,1,4,2,0:T(2,128)}), f32[8,2,1,128,512]{3,1,4,2,0:T(2,128)}, u32[]{:S(2)}, u32[]{:S(2)}) %all-to-all-start) | async-done | bytes 4194336 | tf_op jit(solution)/shard_map/all_to_all | solution.py:54
  68.1 6.6 copy.50
  74.7 5.4 reshape_reshape.6
  81.7 1.4 fusion.58
  83.2 11.7 %cholesky.374 = f32[128,128]{1,0:T(8,128)S(1)} custom-call(f32[128,128]{1,0:T(8,128)S(1)} %cholesky.586), custom_call_target="Cholesky" | custom-call | tf_op jit(solution)/shard_map/jit(cholesky)/cholesky | solution.py:56
  94.9 9.8 %custom-call.35 = f32[1,128,128]{1,2,0:T(8,128)S(1)} custom-call(f32[1,128,128]{2,1,0:T(8,128)S(1)} %get-tuple-element.99), custom_call_target="InvertDiagBlocksLowerTriangular" | custom-call | tf_op jit(solution)/shard_map/jit(cholesky)/cholesky | solution.py:56
  105.6 11.7 %cholesky.393 = f32[128,128]{1,0:T(8,128)S(1)} custom-call(f32[128,128]{1,0:T(8,128)S(1)} %cholesky.590), custom_call_target="Cholesky" | custom-call | tf_op jit(solution)/shard_map/jit(cholesky)/cholesky | solution.py:56
  117.3 10.0 %custom-call.36 = f32[1,128,128]{1,2,0:T(8,128)S(1)} custom-call(f32[1,128,128]{2,1,0:T(8,128)S(1)} %get-tuple-element.96), custom_call_target="InvertDiagBlocksLowerTriangular" | custom-call | tf_op jit(solution)/shard_map/jit(cholesky)/cholesky | solution.py:56
  127.9 11.7 %cholesky.414 = f32[128,128]{1,0:T(8,128)S(1)} custom-call(f32[128,128]{1,0:T(8,128)S(1)} %cholesky.595), custom_call_target="Cholesky" | custom-call | tf_op jit(solution)/shard_map/jit(cholesky)/cholesky | solution.py:56
  140.3 9.8 %custom-call.37 = f32[1,128,128]{1,2,0:T(8,128)S(1)} custom-call(f32[1,128,128]{2,1,0:T(8,128)S(1)} %get-tuple-element.93), custom_call_target="InvertDiagBlocksLowerTriangular" | custom-call | tf_op jit(solution)/shard_map/jit(cholesky)/cholesky | solution.py:56
  150.8 11.7 %cholesky.431 = f32[128,128]{1,0:T(8,128)S(1)} custom-call(f32[128,128]{1,0:T(8,128)S(1)} %convolution_subtract_fusion.15), custom_call_target="Cholesky" | custom-call | tf_op jit(solution)/shard_map/jit(cholesky)/cholesky | solution.py:56
  167.0 7.9 %while.6 = (s32[]{:T(128)}, f32[512,512]{1,0:T(8,128)S(1)}, s32[4,2]{0,1:T(2,128)S(1)}, f32[4,128,128]{2,1,0:T(8,128)S(1)}, s32[]{:T(128)}) while((s32[]{:T(128)}, f32[512,512]{1,0:T(8,128)S(1)}, s32[4,2]{0,1:T(2,128)S(1)}, f32[4,128,128]{2,1,0:T(8,128)S(1)}, s32[]{:T(128)}) %tuple.84), condition=%wide.while_cond, body=%wide.while_body.sunk | while | flops 2 | bytes 131181 | solution.py:57
  174.9 39.3 %custom-call.38 = f32[4,128,128]{1,2,0:T(8,128)S(1)} custom-call(f32[4,128,128]{2,1,0:T(8,128)S(1)} %get-tuple-element.26), custom_call_target="InvertDiagBlocksLowerTriangular" | custom-call | tf_op jit(solution)/shard_map/jit(_solve_triangular)/triangular_solve | solution.py:57
  214.3 2.4 fusion.53
  216.7 2.3 convolution_subtract_fusion.3
  222.3 2.0 fusion.27
  228.1 4.0 fusion.142
  232.4 3.0 stack.7
  235.4 5.3 all-to-all-start.1
  241.8 47.8 %all-to-all-done.1 = f32[8,2,1,128,512]{3,1,4,2,0:T(2,128)} async-done(((f32[8,2,1,128,512]{3,1,4,2,0:T(2,128)}), f32[8,2,1,128,512]{3,1,4,2,0:T(2,128)}, u32[]{:S(2)}, u32[]{:S(2)}) %all-to-all-start.1) | async-done | bytes 4194336 | tf_op jit(solution)/shard_map/all_to_all | solution.py:54
  289.6 6.6 copy.54
  296.2 4.9 reshape_reshape.7
  301.1 2.3 slice.194
  303.4 1.6 copy.55
  304.9 1.4 fusion.57
  307.4 11.7 %cholesky.446 = f32[128,128]{1,0:T(8,128)S(1)} custom-call(f32[128,128]{1,0:T(8,128)S(1)} %cholesky.599), custom_call_target="Cholesky" | custom-call | tf_op jit(solution)/shard_map/jit(cholesky)/cholesky | solution.py:56
  319.2 9.8 %custom-call.39 = f32[1,128,128]{1,2,0:T(8,128)S(1)} custom-call(f32[1,128,128]{2,1,0:T(8,128)S(1)} %get-tuple-element.89), custom_call_target="InvertDiagBlocksLowerTriangular" | custom-call | tf_op jit(solution)/shard_map/jit(cholesky)/cholesky | solution.py:56
  331.6 11.7 %cholesky.465 = f32[128,128]{1,0:T(8,128)S(1)} custom-call(f32[128,128]{1,0:T(8,128)S(1)} %cholesky.603), custom_call_target="Cholesky" | custom-call | tf_op jit(solution)/shard_map/jit(cholesky)/cholesky | solution.py:56
  344.6 10.2 %custom-call.40 = f32[1,128,128]{1,2,0:T(8,128)S(1)} custom-call(f32[1,128,128]{2,1,0:T(8,128)S(1)} %get-tuple-element.86), custom_call_target="InvertDiagBlocksLowerTriangular" | custom-call | tf_op jit(solution)/shard_map/jit(cholesky)/cholesky | solution.py:56
  356.4 11.7 %cholesky.486 = f32[128,128]{1,0:T(8,128)S(1)} custom-call(f32[128,128]{1,0:T(8,128)S(1)} %cholesky.608), custom_call_target="Cholesky" | custom-call | tf_op jit(solution)/shard_map/jit(cholesky)/cholesky | solution.py:56
  368.9 9.8 %custom-call.41 = f32[1,128,128]{1,2,0:T(8,128)S(1)} custom-call(f32[1,128,128]{2,1,0:T(8,128)S(1)} %get-tuple-element.83), custom_call_target="InvertDiagBlocksLowerTriangular" | custom-call | tf_op jit(solution)/shard_map/jit(cholesky)/cholesky | solution.py:56
  380.2 11.7 %cholesky.503 = f32[128,128]{1,0:T(8,128)S(1)} custom-call(f32[128,128]{1,0:T(8,128)S(1)} %convolution_subtract_fusion.14), custom_call_target="Cholesky" | custom-call | tf_op jit(solution)/shard_map/jit(cholesky)/cholesky | solution.py:56
  396.4 11.4 %while.7 = (s32[]{:T(128)}, f32[512,512]{1,0:T(8,128)}, s32[4,2]{0,1:T(2,128)S(1)}, f32[4,128,128]{2,1,0:T(8,128)S(1)}, s32[]{:T(128)}) while((s32[]{:T(128)}, f32[512,512]{1,0:T(8,128)}, s32[4,2]{0,1:T(2,128)S(1)}, f32[4,128,128]{2,1,0:T(8,128)S(1)}, s32[]{:T(128)}) %tuple.97), condition=%wide.while_cond.clone, body=%wide.while_body.clone.sunk | while | flops 2 | bytes 131181 | solution.py:57
  397.0 2.2 bitcast_dynamic-update-slice_fusion.8
  399.9 2.2 bitcast_dynamic-update-slice_fusion.8
  402.7 2.2 bitcast_dynamic-update-slice_fusion.8
  405.6 2.2 bitcast_dynamic-update-slice_fusion.8
  407.7 39.3 %custom-call.42 = f32[4,128,128]{1,2,0:T(8,128)S(1)} custom-call(f32[4,128,128]{2,1,0:T(8,128)S(1)} %get-tuple-element.27), custom_call_target="InvertDiagBlocksLowerTriangular" | custom-call | tf_op jit(solution)/shard_map/jit(_solve_triangular)/triangular_solve | solution.py:57
  447.1 2.4 fusion.51
  449.5 2.3 convolution_subtract_fusion.2
  452.9 2.1 convolution_subtract_fusion
  456.1 3.0 fusion.24
  462.7 1.9 fusion.46
  466.1 1.5 copy.57
  469.2 94.5 %all-gather.5.cloned.1.call-done = bf16[32,128,1024]{2,1,0:T(8,128)(2,1)} async-done(((bf16[1,128,1024]{2,1,0:T(8,128)(2,1)}), bf16[32,128,1024]{2,1,0:T(8,128)(2,1)}) %all-gather.5.cloned.1.call-update) | async-done | bytes 8388624 | tf_op jit(solution)/shard_map/all_gather | solution.py:78
  563.8 8.8 %copy.71 = bf16[512,8,8,128]{3,2,1,0:T(8,128)(2,1)} copy(bf16[512,8,8,128]{3,1,2,0:T(8,128)(2,1)} %bitcast.243) | data formatting | bytes 16777216
  572.5 8.9 %fusion.4 = f32[32,1,128,4,128]{4,3,2,0,1:T(4,128)} fusion(s32[32,8]{1,0:T(8,128)S(1)} %copy.58, bf16[32,128,8,128]{3,2,1,0:T(8,128)(2,1)} %bitcast.234), kind=kOutput, calls=%fused_computation.10 | convolution fusion | flops 33555456 | bytes 16778240 | tf_op jit(solution)/shard_map/muvkc,mkb->muvbc/dot_general | solution.py:20
  581.4 10.3 %reshape.264 = f32[32,128,512]{2,1,0:T(8,128)} reshape(f32[32,1,128,4,128]{4,3,2,0,1:T(4,128)} %fusion.4) | data formatting | bytes 16777216 | tf_op jit(solution)/shard_map/reshape.65
  591.7 10.4 %fusion.2 = f32[4,128,512]{2,0,1:T(4,128)S(1)} fusion(f32[32,128,512]{2,1,0:T(8,128)} %reshape.264, s32[32]{0:T(128)S(1)} %get-tuple-element.108, pred[32]{0:T(512)(128)(4,1)S(1)} %broadcast_compare_fusion), kind=kOutput, calls=%fused_computation.8 | convolution fusion | flops 100663552 | bytes 9437344 | tf_op jit(solution)/shard_map/muvx,mut->tvx/dot_general | solution.py:35
  609.0 24.5 %all-gather.7.cloned.1.call-done = f32[1,1024,512]{1,2,0:T(8,128)} async-done(((f32[1,128,512]{1,2,0:T(8,128)}), f32[1,1024,512]{1,2,0:T(8,128)}) %all-gather.7.cloned.1.call-update) | async-done | bytes 2097168 | tf_op jit(solution)/shard_map/all_gather | solution.py:83
  635.1 1.4 fusion.55
  636.6 11.7 %cholesky.518 = f32[128,128]{1,0:T(8,128)S(1)} custom-call(f32[128,128]{1,0:T(8,128)S(1)} %cholesky.612), custom_call_target="Cholesky" | custom-call | tf_op jit(solution)/shard_map/jit(cholesky)/cholesky | solution.py:84
  648.5 9.8 %custom-call.43 = f32[1,128,128]{1,2,0:T(8,128)S(1)} custom-call(f32[1,128,128]{2,1,0:T(8,128)S(1)} %get-tuple-element.79), custom_call_target="InvertDiagBlocksLowerTriangular" | custom-call | tf_op jit(solution)/shard_map/jit(cholesky)/cholesky | solution.py:84
  659.0 11.7 %cholesky.537 = f32[128,128]{1,0:T(8,128)S(1)} custom-call(f32[128,128]{1,0:T(8,128)S(1)} %cholesky.616), custom_call_target="Cholesky" | custom-call | tf_op jit(solution)/shard_map/jit(cholesky)/cholesky | solution.py:84
  672.1 10.0 %custom-call.44 = f32[1,128,128]{1,2,0:T(8,128)S(1)} custom-call(f32[1,128,128]{2,1,0:T(8,128)S(1)} %get-tuple-element.76), custom_call_target="InvertDiagBlocksLowerTriangular" | custom-call | tf_op jit(solution)/shard_map/jit(cholesky)/cholesky | solution.py:84
  682.7 11.7 %cholesky.558 = f32[128,128]{1,0:T(8,128)S(1)} custom-call(f32[128,128]{1,0:T(8,128)S(1)} %cholesky.621), custom_call_target="Cholesky" | custom-call | tf_op jit(solution)/shard_map/jit(cholesky)/cholesky | solution.py:84
  695.1 9.8 %custom-call.45 = f32[1,128,128]{1,2,0:T(8,128)S(1)} custom-call(f32[1,128,128]{2,1,0:T(8,128)S(1)} %get-tuple-element.73), custom_call_target="InvertDiagBlocksLowerTriangular" | custom-call | tf_op jit(solution)/shard_map/jit(cholesky)/cholesky | solution.py:84
  705.5 11.9 %cholesky.575 = f32[128,128]{1,0:T(8,128)S(1)} custom-call(f32[128,128]{1,0:T(8,128)S(1)} %convolution_subtract_fusion.13), custom_call_target="Cholesky" | custom-call | tf_op jit(solution)/shard_map/jit(cholesky)/cholesky | solution.py:84
  720.8 8.5 %while.5 = (s32[]{:T(128)}, f32[512,512]{1,0:T(8,128)S(1)}, s32[4,2]{0,1:T(2,128)S(1)}, f32[4,128,128]{2,1,0:T(8,128)S(1)}, s32[]{:T(128)}) while((s32[]{:T(128)}, f32[512,512]{1,0:T(8,128)S(1)}, s32[4,2]{0,1:T(2,128)S(1)}, f32[4,128,128]{2,1,0:T(8,128)S(1)}, s32[]{:T(128)}) %tuple.98), condition=%wide.while_cond.1, body=%wide.while_body.1.sunk | while | flops 2 | bytes 131181 | solution.py:86
  721.5 1.4 bitcast_dynamic-update-slice_fusion.6
  723.6 1.4 bitcast_dynamic-update-slice_fusion.6
  729.3 39.3 %custom-call.27 = f32[4,128,128]{1,2,0:T(8,128)S(1)} custom-call(f32[4,128,128]{2,1,0:T(8,128)S(1)} %get-tuple-element.19), custom_call_target="InvertDiagBlocksLowerTriangular" | custom-call | tf_op jit(solution)/shard_map/jit(_solve_triangular)/triangular_solve | solution.py:86
  (166 shorter events, 68.9 us)
Async XLA Ops:
  11.5 56.6 %all-to-all-start = ((f32[8,2,1,128,512]{3,1,4,2,0:T(2,128)}), f32[8,2,1,128,512]{3,1,4,2,0:T(2,128)}, u32[]{:S(2)}, u32[]{:S(2)}) async-start(f32[8,2,1,128,512]{3,1,4,2,0:T(2,128)} %stack.6), calls=%async_computation | async-start | bytes 8388608 | tf_op jit(solution)/shard_map/all_to_all | solution.py:54
  214.3 5.8 copy-start
  226.5 1.6 copy-start.6
  227.8 4.3 copy-start.2
  235.4 54.2 %all-to-all-start.1 = ((f32[8,2,1,128,512]{3,1,4,2,0:T(2,128)}), f32[8,2,1,128,512]{3,1,4,2,0:T(2,128)}, u32[]{:S(2)}, u32[]{:S(2)}) async-start(f32[8,2,1,128,512]{3,1,4,2,0:T(2,128)} %stack.7), calls=%async_computation.1 | async-start | bytes 8388608 | tf_op jit(solution)/shard_map/all_to_all | solution.py:54
  240.7 323.0 %all-gather.5.cloned.1.call-start = ((), (), s32[]{:S(2)}) async-start(), calls=%async_computation.2 | async-start | bytes 8650752 | tf_op jit(solution)/shard_map/all_gather | solution.py:78
  306.4 1.0 copy-start.5
  447.1 5.8 copy-start.1
  462.3 2.4 copy-start.4
  462.3 3.7 copy-start.7
  462.7 5.0 copy-start.8
  462.7 5.0 copy-start.9
  462.7 6.3 copy-start.10
  465.9 167.6 %all-gather.7.cloned.1.call-start = ((), (), s32[]{:S(2)}) async-start(), calls=%async_computation.3 | async-start | bytes 2359296 | tf_op jit(solution)/shard_map/all_gather | solution.py:83
  602.1 3.5 copy-start.3
Sparse Core Ops, SparseCore 0:
  466.1 97.6 all-gather.4
  605.8 27.6 all-gather.6
